TPU v7x, 32 devices: a whole 2x2x4 slice. The times are simulated.
32 devices in a mesh: row: 4 (over z), col: 8 (over y, x, core).
Axes of the slice: x: 2, y: 2, z: 4, core: 2. Of those that a mesh axis runs over, the one named last changes fastest.
Arguments:
- tokens: bfloat16 [256, 8192], P('col', 'row'), may hold values from -6 to 6
- out_grad: bfloat16 [256, 8192], P('col', 'row'), may hold values from -1.1953125 to 1.1953125
- w_gate: bfloat16 [8192, 16384], P('row', 'col'), may hold values from -0.0625 to 0.0625
- w_up: bfloat16 [8192, 16384], P('row', 'col'), may hold values from -0.0625 to 0.0625
- w_down: bfloat16 [16384, 8192], P('col', 'row'), may hold values from -0.046875 to 0.046875
Outputs:
- grad_input: bfloat16 [256, 8192], P('col', 'row')
- grad_gate: bfloat16 [8192, 16384], P('row', 'col')
- grad_up: bfloat16 [8192, 16384], P('row', 'col')
- grad_down: bfloat16 [16384, 8192], P('col', 'row')
All inputs are finite; a program needn't handle non-finite values.
Results may differ from a plain program's by a relative error of at most 0.0049.
Values may be sent and summed in bfloat16 or wider, within the bound.
A program may use at most 128 MiB of HBM per device.

v0:
```python
import jax
import jax.numpy as jnp
from jax import lax
from jax.sharding import PartitionSpec as P


def contract(left_array, right_array, left_dim, right_dim):
    return lax.dot_general(
        left_array,
        right_array,
        (((left_dim,), (right_dim,)), ((), ())),
        preferred_element_type=jnp.float32,
    )


def swiglu_back(gate_sum, up_sum, hidden_grad):
    logistic = jax.nn.sigmoid(gate_sum)
    active = gate_sum * logistic
    hidden = (active * up_sum).astype(jnp.bfloat16)
    up_grad = (hidden_grad * active).astype(jnp.bfloat16)
    gate_grad = (hidden_grad * up_sum * logistic * (1.0 + gate_sum * (1.0 - logistic))).astype(
        jnp.bfloat16
    )
    return (hidden, gate_grad, up_grad)


def shards(tokens, out_grad, w_gate, w_up, w_down):
    all_tokens, all_grads = (
        lax.all_gather(tokens, "col", axis=0, tiled=True),
        lax.all_gather(out_grad, "col", axis=0, tiled=True),
    )
    gate_part = jnp.dot(all_tokens, w_gate, preferred_element_type=jnp.float32)
    up_part = jnp.dot(all_tokens, w_up, preferred_element_type=jnp.float32)
    grad_part = contract(all_grads, w_down, 1, 1)
    gate_sum, up_sum, hidden_grad = lax.psum((gate_part, up_part, grad_part), "row")
    hidden, gate_grad, up_grad = swiglu_back(gate_sum, up_sum, hidden_grad)
    grad_down = contract(hidden, all_grads, 0, 0).astype(jnp.bfloat16)
    grad_gate = contract(all_tokens, gate_grad, 0, 0).astype(jnp.bfloat16)
    grad_up = contract(all_tokens, up_grad, 0, 0).astype(jnp.bfloat16)
    grad_input = lax.psum_scatter(
        contract(gate_grad, w_gate, 1, 1) + contract(up_grad, w_up, 1, 1),
        "col",
        scatter_dimension=0,
        tiled=True,
    ).astype(jnp.bfloat16)
    return (grad_input, grad_gate, grad_up, grad_down)


def solution(mesh):
    return jax.shard_map(
        shards,
        mesh=mesh,
        in_specs=(
            P("col", "row"),
            P("col", "row"),
            P("row", "col"),
            P("row", "col"),
            P("col", "row"),
        ),
        out_specs=(P("col", "row"), P("row", "col"), P("row", "col"), P("col", "row")),
        check_vma=False,
    )
```

profile of v0, /device:TPU:0, one launch (start us, length us, event | category | flops | bytes accessed | tf_op | source)
XLA Modules:
  0.0 358.6 jit_solution(17293567438412855465)
XLA Ops:
  7.2 0.0 all-gather.5.cloned.1.call-start
  7.2 0.7 all-gather.5.cloned.1.call-update
  7.9 0.0 all-gather.3.cloned.1.call-start
  7.9 0.7 all-gather.3.cloned.1.call-update
  8.6 0.0 all-reduce.3.cloned.1.call-start
  8.7 27.4 %all-gather.5.cloned.1.call-done = bf16[256,2048]{1,0:T(8,128)(2,1)} async-done(((bf16[32,2048]{1,0:T(8,128)(2,1)}), bf16[256,2048]{1,0:T(8,128)(2,1)}) %all-gather.5.cloned.1.call-update) | async-done | bytes 1048592 | tf_op jit(solution)/shard_map/all_gather | solution.py:29
  36.1 7.4 %fusion.5 = f32[256,2048]{1,0:T(8,128)} fusion(bf16[256,2048]{1,0:T(8,128)(2,1)} %all-gather.5.cloned.1.call-done, bf16[2048,2048]{1,0:T(8,128)(2,1)} %param.7), kind=kOutput, calls=%fused_computation.12 | convolution fusion | flops 2147483648 | bytes 11534336 | tf_op jit(solution)/shard_map/dot_general | solution.py:32
  43.6 7.2 %fusion.4 = f32[256,2048]{1,0:T(8,128)} fusion(bf16[256,2048]{1,0:T(8,128)(2,1)S(1)} %copy-done, bf16[2048,2048]{1,0:T(8,128)(2,1)} %param.8), kind=kOutput, calls=%fused_computation.11 | convolution fusion | flops 2147483648 | bytes 11534336 | tf_op jit(solution)/shard_map/dot_general | solution.py:33
  50.7 10.8 %all-gather.3.cloned.1.call-done = bf16[256,2048]{1,0:T(8,128)(2,1)} async-done(((bf16[32,2048]{1,0:T(8,128)(2,1)}), bf16[256,2048]{1,0:T(8,128)(2,1)}) %all-gather.3.cloned.1.call-update) | async-done | bytes 1048592 | tf_op jit(solution)/shard_map/all_gather | solution.py:30
  61.5 7.4 %fusion.3 = f32[256,2048]{1,0:T(8,128)} fusion(bf16[256,2048]{1,0:T(8,128)(2,1)} %all-gather.3.cloned.1.call-done, bf16[2048,2048]{1,0:T(8,128)(2,1)} %param.9), kind=kOutput, calls=%fused_computation.10 | convolution fusion | flops 2147483648 | bytes 11534336 | tf_op jit(solution)/shard_map/dot_general | solution.py:8
  68.9 0.0 all-reduce.3.cloned.1.call-update
  68.9 0.2 reduce-scatter.2.cloned.1.call-start
  69.2 223.5 %all-reduce.3.cloned.1.call-done = (f32[256,2048]{1,0:T(8,128)}, f32[256,2048]{1,0:T(8,128)}, f32[256,2048]{1,0:T(8,128)}) async-done(((f32[256,2048]{1,0:T(8,128)}, f32[256,2048]{1,0:T(8,128)}, f32[256,2048]{1,0:T(8,128)}), (f32[256,2048]{1,0:T(8,128)}, f32[256,2048]{1,0:T(8,128)}, f32[256,2048]{1,0:T(8,128)})) %all-reduce.3.cloned.1.call-update) | async-done | bytes 6291472 | tf_op jit(solution)/shard_map/psum | solution.py:35
  292.6 4.3 %multiply_convert_fusion.1 = (bf16[256,2048]{1,0:T(8,128)(2,1)S(1)}, bf16[256,2048]{1,0:T(8,128)(2,1)S(1)}) fusion(f32[256,2048]{1,0:T(8,128)} %get-tuple-element.9, f32[256,2048]{1,0:T(8,128)} %get-tuple-element.8, f32[256,2048]{1,0:T(8,128)} %get-tuple-element.10), kind=kLoop, calls=%fused_computation.5 | loop fusion | flops 6815744 | bytes 8388608 | tf_op jit(solution)/shard_map/convert_element_type | solution.py:20
  297.0 0.0 slice-start.1
  297.0 5.9 %fusion.6 = f32[256,2048]{1,0:T(8,128)S(1)} fusion(bf16[256,2048]{1,0:T(8,128)(2,1)S(1)} %get-tuple-element.12, bf16[2048,2048]{1,0:T(8,128)(2,1)} %param.7), kind=kOutput, calls=%fused_computation.13 | convolution fusion | flops 2147483648 | bytes 11534336 | tf_op jit(solution)/shard_map/dot_general | solution.py:8
  302.9 3.7 %convolution_add_fusion = f32[256,2048]{1,0:T(8,128)} fusion(f32[256,2048]{1,0:T(8,128)S(1)} %fusion.6, bf16[256,2048]{1,0:T(8,128)(2,1)S(1)} %get-tuple-element.11, bf16[2048,2048]{1,0:T(8,128)(2,1)S(1)} %bitcast.20), kind=kOutput, calls=%fused_computation.3 | convolution fusion | flops 2148007936 | bytes 13631488 | tf_op jit(solution)/shard_map/dot_general | solution.py:8
  306.6 0.0 reduce-scatter.2.cloned.1.call-update
  306.6 5.8 %convert_bitcast_fusion.1 = bf16[2048,2048]{0,1:T(8,128)(2,1)} fusion(bf16[256,2048]{1,0:T(8,128)(2,1)S(1)} %get-tuple-element.12, bf16[256,2048]{1,0:T(8,128)(2,1)S(1)} %copy-done), kind=kOutput, calls=%fused_computation.1 | convolution fusion | flops 2151677952 | bytes 10485760 | tf_op jit(solution)/shard_map/dot_general | solution.py:8
  312.4 12.4 %copy.9 = bf16[2048,2048]{1,0:T(8,128)(2,1)} copy(bf16[2048,2048]{0,1:T(8,128)(2,1)} %convert_bitcast_fusion.1) | data formatting | bytes 16777216
  324.8 5.8 %convert_bitcast_fusion = bf16[2048,2048]{0,1:T(8,128)(2,1)} fusion(bf16[256,2048]{1,0:T(8,128)(2,1)S(1)} %get-tuple-element.11, bf16[256,2048]{1,0:T(8,128)(2,1)S(1)} %copy-done), kind=kOutput, calls=%fused_computation | convolution fusion | flops 2151677952 | bytes 10485760 | tf_op jit(solution)/shard_map/dot_general | solution.py:8
  330.6 12.4 %copy.10 = bf16[2048,2048]{1,0:T(8,128)(2,1)} copy(bf16[2048,2048]{0,1:T(8,128)(2,1)} %convert_bitcast_fusion) | data formatting | bytes 16777216
  343.0 7.5 %convolution_convert_fusion = bf16[2048,2048]{1,0:T(8,128)(2,1)} fusion(bf16[256,2048]{1,0:T(8,128)(2,1)S(1)} %copy-done.2, f32[256,2048]{1,0:T(8,128)} %get-tuple-element.10, f32[256,2048]{1,0:T(8,128)S(1)} %copy-done.1), kind=kOutput, calls=%fused_computation.2 | convolution fusion | flops 2154823680 | bytes 13631488 | tf_op jit(solution)/shard_map/dot_general | solution.py:8
  350.5 1.6 convert_element_type.29
  (11 shorter events, 0.0 us)
Async XLA Ops:
  7.2 28.9 %all-gather.5.cloned.1.call-start = ((), (), s32[]{:S(2)}) async-start(), calls=%async_computation.2 | async-start | bytes 1179648 | tf_op jit(solution)/shard_map/all_gather | solution.py:29
  7.9 53.6 %all-gather.3.cloned.1.call-start = ((), (), s32[]{:S(2)}) async-start(), calls=%async_computation.1 | async-start | bytes 1179648 | tf_op jit(solution)/shard_map/all_gather | solution.py:30
  8.6 284.0 %all-reduce.3.cloned.1.call-start = ((), (), s32[]{:S(2)}) async-start(), calls=%async_computation.4 | async-start | bytes 12582912 | tf_op jit(solution)/shard_map/psum | solution.py:35
  36.1 7.4 %copy-start = (bf16[256,2048]{1,0:T(8,128)(2,1)S(1)}, bf16[256,2048]{1,0:T(8,128)(2,1)}, u32[]{:S(2)}) copy-start(bf16[256,2048]{1,0:T(8,128)(2,1)} %all-gather.5.cloned.1.call-done) | copy-start | bytes 3145732
  68.9 281.5 %reduce-scatter.2.cloned.1.call-start = ((), (), s32[]{:S(2)}) async-start(), calls=%async_computation.3 | async-start | bytes 2359296 | tf_op jit(solution)/shard_map/reduce_scatter | solution.py:40
  292.6 10.2 %slice-start = ((s8[8388608]{0:T(1024)(128)(4,1)}), s8[4194304]{0:T(1024)(128)(4,1)S(1)}, s32[]{:S(2)}) async-start(s8[8388608]{0:T(1024)(128)(4,1)} %bitcast.19), calls=%async_computation.5 | async-start | bytes 8388608
  297.0 5.9 %slice-start.1 = ((s8[8388608]{0:T(1024)(128)(4,1)}), s8[4194304]{0:T(1024)(128)(4,1)S(1)}, s32[]{:S(2)}) async-start(s8[8388608]{0:T(1024)(128)(4,1)} %bitcast.19), calls=%async_computation.6 | async-start | bytes 8388608
  330.6 12.4 %copy-start.1 = (f32[256,2048]{1,0:T(8,128)S(1)}, f32[256,2048]{1,0:T(8,128)}, u32[]{:S(2)}) copy-start(f32[256,2048]{1,0:T(8,128)} %get-tuple-element.8) | copy-start | bytes 6291460
  330.6 12.4 %copy-start.2 = (bf16[256,2048]{1,0:T(8,128)(2,1)S(1)}, bf16[256,2048]{1,0:T(8,128)(2,1)}, u32[]{:S(2)}) copy-start(bf16[256,2048]{1,0:T(8,128)(2,1)} %all-gather.3.cloned.1.call-done) | copy-start | bytes 3145732
Sparse Core Ops, SparseCore 0:
  9.9 26.1 all-gather.4
  38.0 23.4 all-gather.2
  69.1 223.5 all-reduce.2
  306.8 40.1 reduce-scatter.1
where the time goes:
time: 359 us
  waiting for transfers between devices  263 us (73%)
  matrix products  50.7 us (14%)
  local copies, waits for them, and re-layouts  24.8 us (7%)
  between operations  13.8 us (4%)
  other arithmetic  5.93 us (2%)
    psum x1, waiting for transfers between devices, shards(): lax.psum((gate_part, up_part, grad_part), 'row')  223 us
    dot_general x6, matrix products, contract(): lax.dot_general(left_array, right_array, (((left_dim,), (right_dim,)), ((...  36 us
    all_gather x1, waiting for transfers between devices, shards(): lax.all_gather(tokens, 'col', axis=0, tiled=True)  27.4 us
    unnamed x12, local copies, waits for them, and re-layouts  24.8 us
    all_gather x1, waiting for transfers between devices, shards(): lax.all_gather(out_grad, 'col', axis=0, tiled=True)  10.8 us
    dot_general x1, matrix products, shards(): gate_part = jnp.dot(all_tokens, w_gate, preferred_element_type=jnp.float32)  7.44 us
  transfers between devices with their start and end apart: 4, of which 3 were waited for; matrix products, arithmetic and copies ran while one was open for 16% of the time, Pallas kernels for 0%

commit v1 on v0

v1 whole, which is shorter than its diff:
```python
import jax
import jax.numpy as jnp
from jax import lax
from jax.experimental import pallas as pl
from jax.experimental.pallas import tpu as pltpu
from jax.sharding import PartitionSpec as P

BF16 = jnp.bfloat16
F32 = jnp.float32


def contract(left_array, right_array, left_dim, right_dim):
    return lax.dot_general(
        left_array,
        right_array,
        (((left_dim,), (right_dim,)), ((), ())),
        preferred_element_type=F32,
    )


def swiglu_back(gate_sum, up_sum, hidden_grad):
    logistic = jax.nn.sigmoid(gate_sum)
    active = gate_sum * logistic
    hidden = (active * up_sum).astype(BF16)
    up_grad = (hidden_grad * active).astype(BF16)
    gate_grad = (hidden_grad * up_sum * logistic * (1.0 + gate_sum * (1.0 - logistic))).astype(BF16)
    return (hidden, gate_grad, up_grad)


def weight_grads_kernel(xt, ht, gg, ug, og, out_gate, out_up, out_down):
    out_gate[...] = jnp.dot(xt[...], gg[...], preferred_element_type=F32).astype(BF16)
    out_up[...] = jnp.dot(xt[...], ug[...], preferred_element_type=F32).astype(BF16)
    out_down[...] = jnp.dot(ht[...], og[...], preferred_element_type=F32).astype(BF16)


def weight_grads(tokens_t, hidden_t, gate_grad, up_grad, all_grads):
    d, t = tokens_t.shape
    f = hidden_t.shape[0]
    steps = 8
    whole = lambda a: pl.BlockSpec(a.shape, lambda i: (0, 0))
    return pl.pallas_call(
        weight_grads_kernel,
        grid=(steps,),
        in_specs=[
            pl.BlockSpec((d // steps, t), lambda i: (i, 0)),
            pl.BlockSpec((f // steps, t), lambda i: (i, 0)),
            whole(gate_grad),
            whole(up_grad),
            whole(all_grads),
        ],
        out_specs=[
            pl.BlockSpec((d // steps, f), lambda i: (i, 0)),
            pl.BlockSpec((d // steps, f), lambda i: (i, 0)),
            pl.BlockSpec((f // steps, d), lambda i: (i, 0)),
        ],
        out_shape=[
            jax.ShapeDtypeStruct((d, f), BF16),
            jax.ShapeDtypeStruct((d, f), BF16),
            jax.ShapeDtypeStruct((f, d), BF16),
        ],
        compiler_params=pltpu.CompilerParams(vmem_limit_bytes=40 * 2**20),
        cost_estimate=pl.CostEstimate(
            flops=6 * t * d * f, bytes_accessed=6 * d * f + 10 * t * d, transcendentals=0
        ),
    )(tokens_t, hidden_t, gate_grad, up_grad, all_grads)


def shards(tokens, out_grad, w_gate, w_up, w_down):
    all_tokens = lax.all_gather(tokens, "col", axis=0, tiled=True)
    all_grads = lax.all_gather(out_grad, "col", axis=0, tiled=True)
    gate_part = jnp.dot(all_tokens, w_gate, preferred_element_type=F32)
    up_part = jnp.dot(all_tokens, w_up, preferred_element_type=F32)
    grad_part = contract(all_grads, w_down, 1, 1)
    scattered = [
        lax.psum_scatter(p, "row", scatter_dimension=0, tiled=True)
        for p in (gate_part, up_part, grad_part)
    ]
    hidden, gate_grad, up_grad = [
        lax.all_gather(v, "row", axis=0, tiled=True) for v in swiglu_back(*scattered)
    ]
    share = contract(gate_grad, w_gate, 1, 1) + contract(up_grad, w_up, 1, 1)
    grad_input = lax.psum_scatter(share, "col", scatter_dimension=0, tiled=True).astype(BF16)
    grad_gate, grad_up, grad_down = weight_grads(
        all_tokens.T, hidden.T, gate_grad, up_grad, all_grads
    )
    return (grad_input, grad_gate, grad_up, grad_down)


def solution(mesh):
    return jax.shard_map(
        shards,
        mesh=mesh,
        in_specs=(
            P("col", "row"),
            P("col", "row"),
            P("row", "col"),
            P("row", "col"),
            P("col", "row"),
        ),
        out_specs=(P("col", "row"), P("row", "col"), P("row", "col"), P("col", "row")),
        check_vma=False,
    )
```

time: 359 us -> 342 us (0.953)
  local copies, waits for them, and re-layouts: 24.8 us -> 4.45 us
  matrix products: 50.7 us -> 37.4 us
  Pallas kernels: 0 us -> 10.9 us
  waiting for transfers between devices: 263 us -> 271 us
    psum x1 -> x0, waiting for transfers between devices: 223 us -> none  [shards(): lax.psum((gate_part, up_part, grad_part), 'row')]
    reduce_scatter x1 -> x4, waiting for transfers between devices: 0.01 us -> 161 us  [the longest x3 131 us: shards(): lax.psum_scatter(p, 'row', scatter_dimension=0, tiled=True)]
    all_gather x2 -> x5, waiting for transfers between devices: 38.2 us -> 107 us  [the longest x3 69.1 us: shards(): lax.all_gather(v, 'row', axis=0, tiled=True)]
    unnamed x12 -> x8, local copies, waits for them, and re-layouts: 24.8 us -> 2.45 us
    dot_general x6 -> x3, matrix products: 36 us -> 22.8 us  [contract(): lax.dot_general(left_array, right_array, (((left_dim,), (right_dim,)), ((...]
    pallas_call x0 -> x1, Pallas kernels: none -> 10.9 us  [weight_grads(): pl.pallas_call(weight_grads_kernel, grid=(steps,), in_specs=[pl.BlockSpec...]
  transfers between devices with their start and end apart: 4 -> 9, of which waited for: 3 -> 9; matrix products, arithmetic and copies ran while one was open for 16% -> 12% of each run, Pallas kernels for 0% -> 3%
where the time goes in v1:
time: 342 us
  waiting for transfers between devices  271 us (79%)
  matrix products  37.4 us (11%)
  between operations  13.9 us (4%)
  Pallas kernels  10.9 us (3%)
  local copies, waits for them, and re-layouts  4.45 us (1%)
  other arithmetic  4.11 us (1%)
    reduce_scatter x3, waiting for transfers between devices, shards(): lax.psum_scatter(p, 'row', scatter_dimension=0, tiled=True)  131 us
    all_gather x3, waiting for transfers between devices, shards(): lax.all_gather(v, 'row', axis=0, tiled=True)  69.1 us
    reduce_scatter x1, waiting for transfers between devices, shards(): lax.psum_scatter(share, 'col', scatter_dimension=0, tiled=True).astype(BF16)  29.6 us
    all_gather x1, waiting for transfers between devices, shards(): all_tokens = lax.all_gather(tokens, 'col', axis=0, tiled=True)  27.4 us
    dot_general x3, matrix products, contract(): lax.dot_general(left_array, right_array, (((left_dim,), (right_dim,)), ((...  22.8 us
    pallas_call x1, Pallas kernels, weight_grads(): pl.pallas_call(weight_grads_kernel, grid=(steps,), in_specs=[pl.BlockSpec...  10.9 us
    all_gather x1, waiting for transfers between devices, shards(): all_grads = lax.all_gather(out_grad, 'col', axis=0, tiled=True)  10.6 us
    dot_general x1, matrix products, shards(): up_part = jnp.dot(all_tokens, w_up, preferred_element_type=F32)  7.44 us
  transfers between devices with their start and end apart: 9, of which 9 were waited for; matrix products, arithmetic and copies ran while one was open for 12% of the time, Pallas kernels for 3%

profile of v1, /device:TPU:0, one launch (start us, length us, event | category | flops | bytes accessed | tf_op | source)
XLA Modules:
  0.0 342.1 jit_solution(1947464987023254496)
XLA Ops:
  7.2 0.7 all-gather.8.cloned.1.call-update
  7.9 0.7 all-gather.6.cloned.1.call-update
  8.7 27.4 %all-gather.8.cloned.1.call-done = bf16[256,2048]{1,0:T(8,128)(2,1)} async-done(((bf16[32,2048]{1,0:T(8,128)(2,1)}), bf16[256,2048]{1,0:T(8,128)(2,1)}) %all-gather.8.cloned.1.call-update) | async-done | bytes 1048592 | tf_op jit(solution)/shard_map/all_gather | solution.py:69
  36.1 7.4 %fusion.2 = f32[256,2048]{1,0:T(8,128)} fusion(bf16[256,2048]{1,0:T(8,128)(2,1)} %all-gather.8.cloned.1.call-done, bf16[2048,2048]{1,0:T(8,128)(2,1)} %param.8), kind=kOutput, calls=%fused_computation.7 | convolution fusion | flops 2147483648 | bytes 11534336 | tf_op jit(solution)/shard_map/dot_general | solution.py:72
  43.6 7.2 %fusion.3 = f32[256,2048]{1,0:T(8,128)} fusion(bf16[256,2048]{1,0:T(8,128)(2,1)S(1)} %copy-done.3, bf16[2048,2048]{1,0:T(8,128)(2,1)} %param.7), kind=kOutput, calls=%fused_computation.8 | convolution fusion | flops 2147483648 | bytes 11534336 | tf_op jit(solution)/shard_map/dot_general | solution.py:71
  50.9 10.6 %all-gather.6.cloned.1.call-done.og = bf16[256,2048]{1,0:T(8,128)(2,1)} async-done(((bf16[32,2048]{1,0:T(8,128)(2,1)}), bf16[256,2048]{1,0:T(8,128)(2,1)}) %all-gather.6.cloned.1.call-update) | async-done | bytes 1048592 | tf_op jit(solution)/shard_map/all_gather | solution.py:70
  61.5 7.4 %fusion.1 = f32[256,2048]{1,0:T(8,128)} fusion(bf16[256,2048]{1,0:T(8,128)(2,1)} %all-gather.6.cloned.1.call-done.og, bf16[2048,2048]{1,0:T(8,128)(2,1)} %param.9), kind=kOutput, calls=%fused_computation.6 | convolution fusion | flops 2147483648 | bytes 11534336 | tf_op jit(solution)/shard_map/dot_general | solution.py:13
  69.0 39.3 %reduce-scatter.7.cloned.1.call-done = f32[64,2048]{1,0:T(8,128)} async-done(((f32[256,2048]{1,0:T(8,128)}), f32[64,2048]{1,0:T(8,128)}) %reduce-scatter.7.cloned.1.call-update) | async-done | bytes 524304 | tf_op jit(solution)/shard_map/reduce_scatter | solution.py:75
  108.3 46.0 %reduce-scatter.9.cloned.1.call-done = f32[64,2048]{1,0:T(8,128)} async-done(((f32[256,2048]{1,0:T(8,128)}), f32[64,2048]{1,0:T(8,128)}) %reduce-scatter.9.cloned.1.call-update) | async-done | bytes 524304 | tf_op jit(solution)/shard_map/reduce_scatter | solution.py:75
  154.3 46.0 %reduce-scatter.5.cloned.1.call-done = f32[64,2048]{1,0:T(8,128)} async-done(((f32[256,2048]{1,0:T(8,128)}), f32[64,2048]{1,0:T(8,128)}) %reduce-scatter.5.cloned.1.call-update) | async-done | bytes 524304 | tf_op jit(solution)/shard_map/reduce_scatter | solution.py:75
  200.3 2.5 multiply_convert_fusion
  202.8 0.7 all-gather.12.cloned.1.call-update
  203.6 0.7 all-gather.14.cloned.1.call-update
  204.5 25.7 %all-gather.10.cloned.1.call-done.gg = bf16[256,2048]{1,0:T(8,128)(2,1)} async-done(((bf16[64,2048]{1,0:T(8,128)(2,1)}), bf16[256,2048]{1,0:T(8,128)(2,1)}) %all-gather.10.cloned.1.call-update) | async-done | bytes 1048592 | tf_op jit(solution)/shard_map/all_gather | solution.py:79
  230.2 7.4 %fusion.4 = f32[256,2048]{1,0:T(8,128)} fusion(bf16[256,2048]{1,0:T(8,128)(2,1)} %all-gather.10.cloned.1.call-done.gg, bf16[2048,2048]{1,0:T(8,128)(2,1)} %param.7), kind=kOutput, calls=%fused_computation.9 | convolution fusion | flops 2147483648 | bytes 11534336 | tf_op jit(solution)/shard_map/dot_general | solution.py:13
  237.6 22.3 %all-gather.12.cloned.1.call-done.ug = bf16[256,2048]{1,0:T(8,128)(2,1)} async-done(((bf16[64,2048]{1,0:T(8,128)(2,1)}), bf16[256,2048]{1,0:T(8,128)(2,1)}) %all-gather.12.cloned.1.call-update) | async-done | bytes 1048592 | tf_op jit(solution)/shard_map/all_gather | solution.py:79
  259.9 8.0 %convolution_add_fusion = f32[256,2048]{1,0:T(8,128)} fusion(f32[256,2048]{1,0:T(8,128)} %fusion.4, bf16[256,2048]{1,0:T(8,128)(2,1)} %all-gather.12.cloned.1.call-done.ug, bf16[2048,2048]{1,0:T(8,128)(2,1)} %param.8), kind=kOutput, calls=%fused_computation | convolution fusion | flops 2148007936 | bytes 13631488 | tf_op jit(solution)/shard_map/dot_general | solution.py:13
  268.4 21.1 %all-gather.14.cloned.1.call-done = bf16[256,2048]{1,0:T(8,128)(2,1)} async-done(((bf16[64,2048]{1,0:T(8,128)(2,1)}), bf16[256,2048]{1,0:T(8,128)(2,1)}) %all-gather.14.cloned.1.call-update) | async-done | bytes 1048592 | tf_op jit(solution)/shard_map/all_gather | solution.py:79
  289.5 1.5 copy.12.ht
  291.0 1.2 copy-done.1
  292.3 1.2 copy-done.2
  293.5 10.9 %shard_map.84 = (bf16[2048,2048]{1,0:T(8,128)(2,1)}, bf16[2048,2048]{1,0:T(8,128)(2,1)}, bf16[2048,2048]{1,0:T(8,128)(2,1)}) custom-call(bf16[2048,256]{1,0:T(8,128)(2,1)S(1)} %bitcast.12, bf16[2048,256]{1,0:T(8,128)(2,1)S(1)} %copy.12.ht, bf16[256,2048]{1,0:T(8,128)(2,1)S(1)} %copy-done.1, bf16[256,2048]{1,0:T(8,128)(2,1)S(1)} %copy-done.2, ...), custom_call_target="tpu_custom_call" | custom-call | flops 6442450944 | bytes 30408704 | tf_op jit(solution)/shard_map/pallas_call | solution.py:41
  304.4 29.6 %reduce-scatter.11.cloned.1.call-done = f32[32,2048]{1,0:T(8,128)} async-done(((f32[256,2048]{1,0:T(8,128)}), f32[32,2048]{1,0:T(8,128)}) %reduce-scatter.11.cloned.1.call-update) | async-done | bytes 262160 | tf_op jit(solution)/shard_map/reduce_scatter | solution.py:82
  333.9 1.6 convert_element_type.14
  (21 shorter events, 1.2 us)
Async XLA Ops:
  7.2 28.9 %all-gather.8.cloned.1.call-start = ((), (), s32[]{:S(2)}) async-start(), calls=%async_computation.6 | async-start | bytes 1179648 | tf_op jit(solution)/shard_map/all_gather | solution.py:69
  7.9 53.6 %all-gather.6.cloned.1.call-start = ((), (), s32[]{:S(2)}) async-start(), calls=%async_computation.4 | async-start | bytes 1179648 | tf_op jit(solution)/shard_map/all_gather | solution.py:70
  8.6 99.6 %reduce-scatter.7.cloned.1.call-start = ((), (), s32[]{:S(2)}) async-start(), calls=%async_computation.7 | async-start | bytes 2621440 | tf_op jit(solution)/shard_map/reduce_scatter | solution.py:75
  36.1 7.5 %copy-start.3 = (bf16[256,2048]{1,0:T(8,128)(2,1)S(1)}, bf16[256,2048]{1,0:T(8,128)(2,1)}, u32[]{:S(2)}) copy-start(bf16[256,2048]{1,0:T(8,128)(2,1)} %all-gather.8.cloned.1.call-done) | copy-start | bytes 3145732
  43.6 110.7 %reduce-scatter.9.cloned.1.call-start = ((), (), s32[]{:S(2)}) async-start(), calls=%async_computation.8 | async-start | bytes 2621440 | tf_op jit(solution)/shard_map/reduce_scatter | solution.py:75
  50.8 149.4 %reduce-scatter.5.cloned.1.call-start = ((), (), s32[]{:S(2)}) async-start(), calls=%async_computation.5 | async-start | bytes 2621440 | tf_op jit(solution)/shard_map/reduce_scatter | solution.py:75
  68.9 161.2 %all-gather.10.cloned.1.call-start = ((), (), s32[]{:S(2)}) async-start(), calls=%async_computation.9 | async-start | bytes 1310720 | tf_op jit(solution)/shard_map/all_gather | solution.py:79
  202.8 57.1 %all-gather.12.cloned.1.call-start = ((), (), s32[]{:S(2)}) async-start(), calls=%async_computation.10 | async-start | bytes 1310720 | tf_op jit(solution)/shard_map/all_gather | solution.py:79
  203.5 86.0 %all-gather.14.cloned.1.call-start = ((), (), s32[]{:S(2)}) async-start(), calls=%async_computation.12 | async-start | bytes 1310720 | tf_op jit(solution)/shard_map/all_gather | solution.py:79
  204.3 129.7 %reduce-scatter.11.cloned.1.call-start = ((), (), s32[]{:S(2)}) async-start(), calls=%async_computation.11 | async-start | bytes 2359296 | tf_op jit(solution)/shard_map/reduce_scatter | solution.py:82
  237.6 53.4 %copy-start = (bf16[256,2048]{1,0:T(8,128)(2,1)S(1)}, bf16[256,2048]{1,0:T(8,128)(2,1)}, u32[]{:S(2)}) copy-start(bf16[256,2048]{1,0:T(8,128)(2,1)} %all-gather.6.cloned.1.call-done.og) | copy-start | bytes 3145732
  291.0 1.2 copy-start.1
  292.3 1.2 copy-start.2
Sparse Core Ops, SparseCore 0:
  9.9 26.1 all-gather.7
  38.0 23.4 all-gather.5
  64.4 43.8 reduce-scatter.6
  111.1 43.1 reduce-scatter.8
  157.0 43.1 reduce-scatter.4
  202.9 27.2 all-gather.9
  232.4 27.4 all-gather.11
  262.1 27.4 all-gather.13
  293.2 40.7 reduce-scatter.10

commit v2 on v1

--- a/solution.py
+++ b/solution.py
@@ -1,3 +1,5 @@
+import functools
+
 import jax
 import jax.numpy as jnp
 from jax import lax
@@ -25,6 +27,247 @@
     up_grad = (hidden_grad * active).astype(BF16)
     gate_grad = (hidden_grad * up_sum * logistic * (1.0 + gate_sum * (1.0 - logistic))).astype(BF16)
     return (hidden, gate_grad, up_grad)
+
+
+def forward_kernel(
+    n, ncol, cw, tbs, lag,
+    x_ref, g_ref, wg_hbm, wu_hbm, wd_hbm,
+    xa, ga, out,
+    wg, wu, wd, part, sent, got,
+    w_sem, own_sem, ag_send, ag_recv, re_send, re_recv, up_send, up_recv, dn_send, dn_recv,
+):
+    row, col = lax.axis_index("row"), lax.axis_index("col")
+    tl = x_ref.shape[0]
+    t, f = out.shape[1], out.shape[2]
+    per_half = f // 2 // cw
+    tb = t // tbs
+    chunks = per_half * tb
+    peers = ncol // 2
+    core = lax.rem(col, 2)
+    sibling = col + 1 - 2 * core
+    mesh_id = pl.DeviceIdType.MESH
+
+    def weight_copies(b):
+        cols = pl.ds(pl.multiple_of(b * cw, cw), cw)
+        return (
+            pltpu.make_async_copy(wg_hbm.at[:, cols], wg.at[:, cols], w_sem.at[0, b]),
+            pltpu.make_async_copy(wu_hbm.at[:, cols], wu.at[:, cols], w_sem.at[1, b]),
+            pltpu.make_async_copy(wd_hbm.at[cols, :], wd.at[cols, :], w_sem.at[2, b]),
+        )
+
+    for c in range(per_half):
+        for b in (c, per_half + c):
+            for copy in weight_copies(b):
+                copy.start()
+
+    def peer(j):
+        return lax.rem(col + 2 * j, ncol)
+
+    def rows_of(device):
+        return pl.ds(pl.multiple_of(device * tl, tl), tl)
+
+    barrier = pltpu.get_barrier_semaphore()
+    pl.semaphore_signal(barrier, inc=1, device_id=(row, sibling), device_id_type=mesh_id)
+    for j in range(1, peers):
+        pl.semaphore_signal(barrier, inc=1, device_id=(row, peer(j)), device_id_type=mesh_id)
+
+    for near in (lax.rem(row + 1, n), lax.rem(row + n - 1, n)):
+        pl.semaphore_signal(barrier, inc=1, device_id=(near, col), device_id_type=mesh_id)
+    pl.semaphore_wait(barrier, peers + 2)
+
+    def first_copy(a, j):
+        src, dst = ((x_ref, xa), (g_ref, ga))[a]
+        return pltpu.make_async_remote_copy(
+            src_ref=src,
+            dst_ref=dst.at[rows_of(col), :],
+            send_sem=ag_send.at[a, j],
+            recv_sem=ag_recv.at[a, j],
+            device_id=(row, sibling if j == 0 else peer(j)),
+            device_id_type=mesh_id,
+        )
+
+    def relay_copy(a, j):
+        dst = (xa, ga)[a]
+        block = dst.at[rows_of(lax.rem(col + ncol - 2 * j, ncol)), :]
+        return pltpu.make_async_remote_copy(
+            src_ref=block,
+            dst_ref=block,
+            send_sem=re_send.at[a, j],
+            recv_sem=re_recv.at[a, j],
+            device_id=(row, sibling),
+            device_id_type=mesh_id,
+        )
+
+    own = [
+        pltpu.make_async_copy(src, dst.at[rows_of(col), :], own_sem.at[a])
+        for a, (src, dst) in enumerate(((x_ref, xa), (g_ref, ga)))
+    ]
+    for a in range(2):
+        for j in range(1, peers):
+            first_copy(a, j).start()
+        first_copy(a, 0).start()
+        own[a].start()
+    for a in range(2):
+        for j in range(1, peers):
+            first_copy(a, j).wait_recv()
+            relay_copy(a, j).start()
+    for a in range(2):
+        own[a].wait()
+        first_copy(a, 0).wait_recv()
+        for j in range(1, peers):
+            relay_copy(a, j).wait_recv()
+
+    places = (row, n - 1 - row)
+    ups = (row + 1, row - 1)
+    downs = (row - 1, row + 1)
+
+    def spot(h, k):
+        b = h * per_half + k // tb
+        r = pl.ds(pl.multiple_of(lax.rem(k, tb) * tbs, tbs), tbs)
+        return b, r, pl.ds(pl.multiple_of(b * cw, cw), cw)
+
+    def up_copy(h, k):
+        return pltpu.make_async_remote_copy(
+            src_ref=sent.at[h, k],
+            dst_ref=got.at[h, k],
+            send_sem=up_send.at[h, k],
+            recv_sem=up_recv.at[h, k],
+            device_id=(ups[h], col),
+            device_id_type=mesh_id,
+        )
+
+    def down_copy(h, k):
+        _, r, c = spot(h, k)
+        return pltpu.make_async_remote_copy(
+            src_ref=out.at[:, r, c],
+            dst_ref=out.at[:, r, c],
+            send_sem=dn_send.at[h, k],
+            recv_sem=dn_recv.at[h, k],
+            device_id=(downs[h], col),
+            device_id_type=mesh_id,
+        )
+
+    def reduce_chunk(h, k):
+        place = places[h]
+        b, r, c = spot(h, k)
+
+        @pl.when(place > 0)
+        def _():
+            up_copy(h, k).wait_recv()
+            for i in range(3):
+                part[b, i, r, :] += got[h, k, i].astype(F32)
+
+        @pl.when(place < n - 1)
+        def _():
+            for i in range(3):
+                sent[h, k, i] = part[b, i, r, :].astype(BF16)
+            up_copy(h, k).start()
+
+        @pl.when(place == n - 1)
+        def _():
+            values = swiglu_back(part[b, 0, r, :], part[b, 1, r, :], part[b, 2, r, :])
+            for i in range(3):
+                out[i, r, c] = values[i]
+            down_copy(h, k).start()
+
+    def step(s, carry):
+        @pl.when((s < chunks) & (lax.rem(s, tb) == 0))
+        def _():
+            for h in range(2):
+                b = h * per_half + s // tb
+                for copy in weight_copies(b):
+                    copy.wait()
+                cols = pl.ds(pl.multiple_of(b * cw, cw), cw)
+                part[b, 0] = jnp.dot(xa[...], wg[:, cols], preferred_element_type=F32)
+                part[b, 1] = jnp.dot(xa[...], wu[:, cols], preferred_element_type=F32)
+                part[b, 2] = contract(ga[...], wd[cols, :], 1, 1)
+
+        for h in range(2):
+            k = s - lag * places[h]
+
+            @pl.when((k >= 0) & (k < chunks))
+            def _():
+                reduce_chunk(h, k)
+
+        for h in range(2):
+            k = s - lag * (2 * (n - 1) - places[h])
+
+            @pl.when((k >= 0) & (k < chunks) & (places[h] < n - 1))
+            def _():
+                down_copy(h, k).wait_recv()
+
+                @pl.when(places[h] > 0)
+                def _():
+                    down_copy(h, k).start()
+
+        return carry
+
+    lax.fori_loop(0, chunks + 2 * lag * (n - 1), step, 0)
+
+    for a in range(2):
+        for j in range(peers):
+            first_copy(a, j).wait_send()
+            if j:
+                relay_copy(a, j).wait_send()
+
+    def drain(k, carry):
+        for h in range(2):
+
+            @pl.when(places[h] < n - 1)
+            def _():
+                up_copy(h, k).wait_send()
+
+            @pl.when(places[h] > 0)
+            def _():
+                down_copy(h, k).wait_send()
+
+        return carry
+
+    lax.fori_loop(0, chunks, drain, 0)
+
+
+def forward(n, ncol, tokens, out_grad, w_gate, w_up, w_down):
+    tl, d = tokens.shape
+    f = w_gate.shape[1]
+    t = tl * ncol
+    cw = min(256, f // 2)
+    tbs, lag = 64, 2
+    chunks = f // 2 // cw * (t // tbs)
+    blocks = f // cw
+    vmem = pl.BlockSpec(memory_space=pltpu.VMEM)
+    hbm = pl.BlockSpec(memory_space=pl.ANY)
+    dma = pltpu.SemaphoreType.DMA
+    return pl.pallas_call(
+        functools.partial(forward_kernel, n, ncol, cw, tbs, lag),
+        out_shape=[
+            jax.ShapeDtypeStruct((t, d), BF16),
+            jax.ShapeDtypeStruct((t, d), BF16),
+            jax.ShapeDtypeStruct((3, t, f), BF16),
+        ],
+        in_specs=[vmem, vmem, hbm, hbm, hbm],
+        out_specs=[vmem, vmem, vmem],
+        scratch_shapes=[
+            pltpu.VMEM((d, f), BF16),
+            pltpu.VMEM((d, f), BF16),
+            pltpu.VMEM((f, d), BF16),
+            pltpu.VMEM((blocks, 3, t, cw), F32),
+            pltpu.VMEM((2, chunks, 3, tbs, cw), BF16),
+            pltpu.VMEM((2, chunks, 3, tbs, cw), BF16),
+            dma((3, blocks)),
+            dma((2,)),
+            dma((2, ncol // 2)),
+            dma((2, ncol // 2)),
+            dma((2, ncol // 2)),
+            dma((2, ncol // 2)),
+            dma((2, chunks)),
+            dma((2, chunks)),
+            dma((2, chunks)),
+            dma((2, chunks)),
+        ],
+        compiler_params=pltpu.CompilerParams(
+            collective_id=0, has_side_effects=True, vmem_limit_bytes=58 * 2**20
+        ),
+    )(tokens, out_grad, w_gate, w_up, w_down)
 
 
 def weight_grads_kernel(xt, ht, gg, ug, og, out_gate, out_up, out_down):
@@ -65,19 +308,9 @@
     )(tokens_t, hidden_t, gate_grad, up_grad, all_grads)
 
 
-def shards(tokens, out_grad, w_gate, w_up, w_down):
-    all_tokens = lax.all_gather(tokens, "col", axis=0, tiled=True)
-    all_grads = lax.all_gather(out_grad, "col", axis=0, tiled=True)
-    gate_part = jnp.dot(all_tokens, w_gate, preferred_element_type=F32)
-    up_part = jnp.dot(all_tokens, w_up, preferred_element_type=F32)
-    grad_part = contract(all_grads, w_down, 1, 1)
-    scattered = [
-        lax.psum_scatter(p, "row", scatter_dimension=0, tiled=True)
-        for p in (gate_part, up_part, grad_part)
-    ]
-    hidden, gate_grad, up_grad = [
-        lax.all_gather(v, "row", axis=0, tiled=True) for v in swiglu_back(*scattered)
-    ]
+def shards(n, ncol, tokens, out_grad, w_gate, w_up, w_down):
+    all_tokens, all_grads, results = forward(n, ncol, tokens, out_grad, w_gate, w_up, w_down)
+    hidden, gate_grad, up_grad = results[0], results[1], results[2]
     share = contract(gate_grad, w_gate, 1, 1) + contract(up_grad, w_up, 1, 1)
     grad_input = lax.psum_scatter(share, "col", scatter_dimension=0, tiled=True).astype(BF16)
     grad_gate, grad_up, grad_down = weight_grads(
@@ -88,7 +321,7 @@
 
 def solution(mesh):
     return jax.shard_map(
-        shards,
+        functools.partial(shards, mesh.shape["row"], mesh.shape["col"]),
         mesh=mesh,
         in_specs=(
             P("col", "row"),

time: 342 us -> 176 us (0.51)
  waiting for transfers between devices: 271 us -> 22.4 us
  Pallas kernels: 10.9 us -> 120 us
  matrix products: 37.4 us -> 9.91 us
  local copies, waits for them, and re-layouts: 4.45 us -> 8.44 us
    reduce_scatter x3 -> x0, waiting for transfers between devices: 131 us -> none  [shards(): lax.psum_scatter(p, 'row', scatter_dimension=0, tiled=True)]
    pallas_call x0 -> x1, Pallas kernels: none -> 109 us  [forward(): pl.pallas_call(functools.partial(forward_kernel, n, ncol, cw, tbs, lag),...]
    all_gather x5 -> x0, waiting for transfers between devices: 107 us -> none  [the longest x3 69.1 us: shards(): lax.all_gather(v, 'row', axis=0, tiled=True)]
    dot_general x2 -> x0, matrix products: 14.6 us -> none  [the longest x1 7.44 us: shards(): up_part = jnp.dot(all_tokens, w_up, preferred_element_type=F32)]
    dot_general x3 -> x2, matrix products: 22.8 us -> 9.91 us  [contract(): lax.dot_general(left_array, right_array, (((left_dim,), (right_dim,)), ((...]
    reduce_scatter x1, waiting for transfers between devices: 29.6 us -> 22.4 us  [shards(): lax.psum_scatter(share, 'col', scatter_dimension=0, tiled=True).astype(BF16)]
    pallas_call x0 -> x2, local copies, waits for them, and re-layouts: none -> 4.26 us  [forward(): pl.pallas_call(functools.partial(forward_kernel, n, ncol, cw, tbs, lag),...]
  transfers between devices with their start and end apart: 9 -> 1, of which waited for: 9 -> 1; matrix products, arithmetic and copies ran while one was open for 12% -> 4% of each run, Pallas kernels for 3% -> 6%
where the time goes in v2:
time: 176 us
  Pallas kernels  120 us (68%)
  waiting for transfers between devices  22.4 us (13%)
  between operations  14.1 us (8%)
  matrix products  9.91 us (6%)
  local copies, waits for them, and re-layouts  8.44 us (5%)
    pallas_call x1, Pallas kernels, forward(): pl.pallas_call(functools.partial(forward_kernel, n, ncol, cw, tbs, lag),...  109 us
    reduce_scatter x1, waiting for transfers between devices, shards(): lax.psum_scatter(share, 'col', scatter_dimension=0, tiled=True).astype(BF16)  22.4 us
    pallas_call x1, Pallas kernels, weight_grads(): pl.pallas_call(weight_grads_kernel, grid=(steps,), in_specs=[pl.BlockSpec...  10.9 us
    dot_general x2, matrix products, contract(): lax.dot_general(left_array, right_array, (((left_dim,), (right_dim,)), ((...  9.91 us
    pallas_call x2, local copies, waits for them, and re-layouts, forward(): pl.pallas_call(functools.partial(forward_kernel, n, ncol, cw, tbs, lag),...  4.26 us
  transfers between devices with their start and end apart: 1, of which 1 were waited for; matrix products, arithmetic and copies ran while one was open for 4% of the time, Pallas kernels for 6%

profile of v2, /device:TPU:0, one launch (start us, length us, event | category | flops | bytes accessed | tf_op | source)
XLA Modules:
  0.0 176.1 jit_solution(15848109642004943857)
XLA Ops:
  7.2 0.0 reduce-scatter.2.cloned.1.call-start
  7.2 108.7 %shard_map.84 = (bf16[256,2048]{1,0:T(8,128)(2,1)}, bf16[256,2048]{1,0:T(8,128)(2,1)}, bf16[3,256,2048]{2,1,0:T(8,128)(2,1)}) custom-call(bf16[32,2048]{1,0:T(8,128)(2,1)} %x_ref.1, bf16[32,2048]{1,0:T(8,128)(2,1)} %g_ref.1, bf16[2048,2048]{1,0:T(8,128)(2,1)} %wg_hbm.1, bf16[2048,2048]{1,0:T(8,128)(2,1)} %wu_hbm.1, bf16[2048,2048]{1,0:T(8,128)(2,1)} %wd_hbm.1), custom_call_target="tpu_custom_call" | custom-call | tf_op jit(solution)/shard_map/pallas_call | solution.py:240
  115.9 0.0 copy-start.1
  115.9 0.0 copy-start.2
  116.0 6.2 %fusion = f32[256,2048]{1,0:T(8,128)S(1)} fusion(bf16[2048,2048]{1,0:T(8,128)(2,1)} %wg_hbm.1, bf16[3,256,2048]{2,1,0:T(8,128)(2,1)} %get-tuple-element.10), kind=kOutput, calls=%fused_computation.4 | convolution fusion | flops 2147483648 | bytes 11534336 | tf_op jit(solution)/shard_map/dot_general | solution.py:15
  122.2 0.0 copy-done.1
  122.2 0.8 copy-done.2
  123.0 3.7 %convolution_add_fusion = f32[256,2048]{1,0:T(8,128)} fusion(f32[256,2048]{1,0:T(8,128)S(1)} %fusion, bf16[2048,2048]{1,0:T(8,128)(2,1)S(1)} %copy-done.2, bf16[3,256,2048]{2,1,0:T(8,128)(2,1)S(1)} %copy-done.1), kind=kOutput, calls=%fused_computation | convolution fusion | flops 2148007936 | bytes 13631488 | tf_op jit(solution)/shard_map/dot_general | solution.py:15
  126.7 0.0 reduce-scatter.2.cloned.1.call-update
  126.7 2.8 %copy.10 = bf16[3,256,2048]{1,2,0:T(8,128)(2,1)} copy(bf16[3,256,2048]{2,1,0:T(8,128)(2,1)S(1)} %copy-done.1) | data formatting | bytes 6291456 | tf_op jit(solution)/shard_map/pallas_call | solution.py:240
  129.5 1.5 copy.9
  131.0 0.0 copy-start
  131.0 1.5 slice_bitcast_fusion.ht
  132.5 1.9 %slice_bitcast_fusion.1 = (bf16[256,2048]{1,0:T(8,128)(2,1)S(1)}, bf16[256,2048]{1,0:T(8,128)(2,1)S(1)}) fusion(bf16[3,256,2048]{2,1,0:T(8,128)(2,1)} %get-tuple-element.10), kind=kLoop, calls=%fused_computation.2 | loop fusion | bytes 4194304 | tf_op jit(solution)/shard_map/squeeze | solution.py:313
  134.4 0.0 copy-done
  134.4 10.9 %shard_map.85 = (bf16[2048,2048]{1,0:T(8,128)(2,1)}, bf16[2048,2048]{1,0:T(8,128)(2,1)}, bf16[2048,2048]{1,0:T(8,128)(2,1)}) custom-call(bf16[2048,256]{1,0:T(8,128)(2,1)S(1)} %bitcast.13, bf16[2048,256]{1,0:T(8,128)(2,1)S(1)} %slice_bitcast_fusion.ht, bf16[256,2048]{1,0:T(8,128)(2,1)S(1)} %get-tuple-element.17.gg, ...), custom_call_target="tpu_custom_call" | custom-call | flops 6442450944 | bytes 30408704 | tf_op jit(solution)/shard_map/pallas_call | solution.py:284
  145.3 22.4 %reduce-scatter.2.cloned.1.call-done = f32[32,2048]{1,0:T(8,128)} async-done(((f32[256,2048]{1,0:T(8,128)}), f32[32,2048]{1,0:T(8,128)}) %reduce-scatter.2.cloned.1.call-update) | async-done | bytes 262160 | tf_op jit(solution)/shard_map/reduce_scatter | solution.py:315
  167.7 1.6 convert_element_type.3
Async XLA Ops:
  7.2 160.5 %reduce-scatter.2.cloned.1.call-start = ((), (), s32[]{:S(2)}) async-start(), calls=%async_computation.1 | async-start | bytes 2359296 | tf_op jit(solution)/shard_map/reduce_scatter | solution.py:315
  115.9 6.2 %copy-start.1 = (bf16[3,256,2048]{2,1,0:T(8,128)(2,1)S(1)}, bf16[3,256,2048]{2,1,0:T(8,128)(2,1)}, u32[]{:S(2)}) copy-start(bf16[3,256,2048]{2,1,0:T(8,128)(2,1)} %get-tuple-element.10) | copy-start | bytes 9437188
  115.9 7.0 %copy-start.2 = (bf16[2048,2048]{1,0:T(8,128)(2,1)S(1)}, bf16[2048,2048]{1,0:T(8,128)(2,1)}, u32[]{:S(2)}) copy-start(bf16[2048,2048]{1,0:T(8,128)(2,1)} %wu_hbm.1) | copy-start | bytes 25165828
  131.0 3.4 %copy-start = (bf16[256,2048]{1,0:T(8,128)(2,1)S(1)}, bf16[256,2048]{1,0:T(8,128)(2,1)}, u32[]{:S(2)}) copy-start(bf16[256,2048]{1,0:T(8,128)(2,1)} %get-tuple-element.12.og) | copy-start | bytes 3145732
Sparse Core Ops, SparseCore 0:
  126.8 40.8 reduce-scatter.1

commit v3 on v2

--- a/solution.py
+++ b/solution.py
@@ -126,24 +126,27 @@
         r = pl.ds(pl.multiple_of(lax.rem(k, tb) * tbs, tbs), tbs)
         return b, r, pl.ds(pl.multiple_of(b * cw, cw), cw)
 
-    def up_copy(h, k):
+    root = n // 2
+    away = [jnp.where(place > root, place - root, root - place) for place in places]
+
+    def up_copy(h, k, side):
         return pltpu.make_async_remote_copy(
             src_ref=sent.at[h, k],
-            dst_ref=got.at[h, k],
-            send_sem=up_send.at[h, k],
-            recv_sem=up_recv.at[h, k],
-            device_id=(ups[h], col),
+            dst_ref=got.at[side, h, k],
+            send_sem=up_send.at[side, h, k],
+            recv_sem=up_recv.at[side, h, k],
+            device_id=((ups, downs)[side][h], col),
             device_id_type=mesh_id,
         )
 
-    def down_copy(h, k):
+    def down_copy(h, k, side):
         _, r, c = spot(h, k)
         return pltpu.make_async_remote_copy(
             src_ref=out.at[:, r, c],
             dst_ref=out.at[:, r, c],
-            send_sem=dn_send.at[h, k],
-            recv_sem=dn_recv.at[h, k],
-            device_id=(downs[h], col),
+            send_sem=dn_send.at[side, h, k],
+            recv_sem=dn_recv.at[side, h, k],
+            device_id=((downs, ups)[side][h], col),
             device_id_type=mesh_id,
         )
 
@@ -151,24 +154,31 @@
         place = places[h]
         b, r, c = spot(h, k)
 
-        @pl.when(place > 0)
-        def _():
-            up_copy(h, k).wait_recv()
-            for i in range(3):
-                part[b, i, r, :] += got[h, k, i].astype(F32)
-
-        @pl.when(place < n - 1)
-        def _():
-            for i in range(3):
-                sent[h, k, i] = part[b, i, r, :].astype(BF16)
-            up_copy(h, k).start()
-
-        @pl.when(place == n - 1)
+        for side, inner in enumerate(
+            ((place > 0) & (place <= root), (place >= root) & (place < n - 1))
+        ):
+
+            @pl.when(inner)
+            def _(side=side):
+                up_copy(h, k, side).wait_recv()
+                for i in range(3):
+                    part[b, i, r, :] += got[side, h, k, i].astype(F32)
+
+        for side, outer in enumerate((place < root, place > root)):
+
+            @pl.when(outer)
+            def _(side=side):
+                for i in range(3):
+                    sent[h, k, i] = part[b, i, r, :].astype(BF16)
+                up_copy(h, k, side).start()
+
+        @pl.when(place == root)
         def _():
             values = swiglu_back(part[b, 0, r, :], part[b, 1, r, :], part[b, 2, r, :])
             for i in range(3):
                 out[i, r, c] = values[i]
-            down_copy(h, k).start()
+            down_copy(h, k, 0).start()
+            down_copy(h, k, 1).start()
 
     def step(s, carry):
         @pl.when((s < chunks) & (lax.rem(s, tb) == 0))
@@ -183,26 +193,31 @@
                 part[b, 2] = contract(ga[...], wd[cols, :], 1, 1)
 
         for h in range(2):
-            k = s - lag * places[h]
+            k = s - lag * (root - away[h])
 
             @pl.when((k >= 0) & (k < chunks))
             def _():
                 reduce_chunk(h, k)
 
         for h in range(2):
-            k = s - lag * (2 * (n - 1) - places[h])
-
-            @pl.when((k >= 0) & (k < chunks) & (places[h] < n - 1))
-            def _():
-                down_copy(h, k).wait_recv()
-
-                @pl.when(places[h] > 0)
-                def _():
-                    down_copy(h, k).start()
+            k = s - lag * (root + away[h])
+            place = places[h]
+            for side, outer, inner in (
+                (0, place < root, place > 0),
+                (1, place > root, place < n - 1),
+            ):
+
+                @pl.when((k >= 0) & (k < chunks) & outer)
+                def _(h=h, k=k, side=side, inner=inner):
+                    down_copy(h, k, side).wait_recv()
+
+                    @pl.when(inner)
+                    def _():
+                        down_copy(h, k, side).start()
 
         return carry
 
-    lax.fori_loop(0, chunks + 2 * lag * (n - 1), step, 0)
+    lax.fori_loop(0, chunks + 2 * lag * root, step, 0)
 
     for a in range(2):
         for j in range(peers):
@@ -212,14 +227,19 @@
 
     def drain(k, carry):
         for h in range(2):
-
-            @pl.when(places[h] < n - 1)
-            def _():
-                up_copy(h, k).wait_send()
-
-            @pl.when(places[h] > 0)
-            def _():
-                down_copy(h, k).wait_send()
+            place = places[h]
+            for side, outer, inner in (
+                (0, place < root, (place <= root) & (place > 0)),
+                (1, place > root, (place >= root) & (place < n - 1)),
+            ):
+
+                @pl.when(outer)
+                def _(h=h, side=side):
+                    up_copy(h, k, side).wait_send()
+
+                @pl.when(inner)
+                def _(h=h, side=side):
+                    down_copy(h, k, side).wait_send()
 
         return carry
 
@@ -252,17 +272,17 @@
             pltpu.VMEM((f, d), BF16),
             pltpu.VMEM((blocks, 3, t, cw), F32),
             pltpu.VMEM((2, chunks, 3, tbs, cw), BF16),
-            pltpu.VMEM((2, chunks, 3, tbs, cw), BF16),
+            pltpu.VMEM((2, 2, chunks, 3, tbs, cw), BF16),
             dma((3, blocks)),
             dma((2,)),
             dma((2, ncol // 2)),
             dma((2, ncol // 2)),
             dma((2, ncol // 2)),
             dma((2, ncol // 2)),
-            dma((2, chunks)),
-            dma((2, chunks)),
-            dma((2, chunks)),
-            dma((2, chunks)),
+            dma((2, 2, chunks)),
+            dma((2, 2, chunks)),
+            dma((2, 2, chunks)),
+            dma((2, 2, chunks)),
         ],
         compiler_params=pltpu.CompilerParams(
             collective_id=0, has_side_effects=True, vmem_limit_bytes=58 * 2**20

time: 176 us -> 177 us (level)
  Pallas kernels: 120 us -> 122 us
    pallas_call x1, Pallas kernels: 109 us -> 111 us  [forward(): pl.pallas_call(functools.partial(forward_kernel, n, ncol, cw, tbs, lag),...]
where the time goes in v3:
time: 177 us
  Pallas kernels  122 us (69%)
  waiting for transfers between devices  21.3 us (12%)
  between operations  14.1 us (8%)
  matrix products  9.91 us (6%)
  local copies, waits for them, and re-layouts  8.38 us (5%)
    pallas_call x1, Pallas kernels, forward(): pl.pallas_call(functools.partial(forward_kernel, n, ncol, cw, tbs, lag),...  111 us
    reduce_scatter x1, waiting for transfers between devices, shards(): lax.psum_scatter(share, 'col', scatter_dimension=0, tiled=True).astype(BF16)  21.2 us
    pallas_call x1, Pallas kernels, weight_grads(): pl.pallas_call(weight_grads_kernel, grid=(steps,), in_specs=[pl.BlockSpec...  10.9 us
    dot_general x2, matrix products, contract(): lax.dot_general(left_array, right_array, (((left_dim,), (right_dim,)), ((...  9.91 us
    pallas_call x2, local copies, waits for them, and re-layouts, forward(): pl.pallas_call(functools.partial(forward_kernel, n, ncol, cw, tbs, lag),...  4.28 us
  transfers between devices with their start and end apart: 1, of which 1 were waited for; matrix products, arithmetic and copies ran while one was open for 4% of the time, Pallas kernels for 6%

profile of v3, /device:TPU:0, one launch (start us, length us, event | category | flops | bytes accessed | tf_op | source)
XLA Modules:
  0.0 176.9 jit_solution(531818370669307974)
XLA Ops:
  7.2 0.0 reduce-scatter.2.cloned.1.call-start
  7.2 110.7 %shard_map.84 = (bf16[256,2048]{1,0:T(8,128)(2,1)}, bf16[256,2048]{1,0:T(8,128)(2,1)}, bf16[3,256,2048]{2,1,0:T(8,128)(2,1)}) custom-call(bf16[32,2048]{1,0:T(8,128)(2,1)} %x_ref.1, bf16[32,2048]{1,0:T(8,128)(2,1)} %g_ref.1, bf16[2048,2048]{1,0:T(8,128)(2,1)} %wg_hbm.1, bf16[2048,2048]{1,0:T(8,128)(2,1)} %wu_hbm.1, bf16[2048,2048]{1,0:T(8,128)(2,1)} %wd_hbm.1), custom_call_target="tpu_custom_call" | custom-call | tf_op jit(solution)/shard_map/pallas_call | solution.py:260
  117.9 0.0 copy-start.1
  117.9 0.0 copy-start.2
  117.9 6.2 %fusion = f32[256,2048]{1,0:T(8,128)S(1)} fusion(bf16[2048,2048]{1,0:T(8,128)(2,1)} %wg_hbm.1, bf16[3,256,2048]{2,1,0:T(8,128)(2,1)} %get-tuple-element.10), kind=kOutput, calls=%fused_computation.4 | convolution fusion | flops 2147483648 | bytes 11534336 | tf_op jit(solution)/shard_map/dot_general | solution.py:15
  124.1 0.0 copy-done.1
  124.1 0.8 copy-done.2
  124.9 3.7 %convolution_add_fusion = f32[256,2048]{1,0:T(8,128)} fusion(f32[256,2048]{1,0:T(8,128)S(1)} %fusion, bf16[2048,2048]{1,0:T(8,128)(2,1)S(1)} %copy-done.2, bf16[3,256,2048]{2,1,0:T(8,128)(2,1)S(1)} %copy-done.1), kind=kOutput, calls=%fused_computation | convolution fusion | flops 2148007936 | bytes 13631488 | tf_op jit(solution)/shard_map/dot_general | solution.py:15
  128.6 0.0 reduce-scatter.2.cloned.1.call-update
  128.7 2.8 %copy.10 = bf16[3,256,2048]{1,2,0:T(8,128)(2,1)} copy(bf16[3,256,2048]{2,1,0:T(8,128)(2,1)S(1)} %copy-done.1) | data formatting | bytes 6291456 | tf_op jit(solution)/shard_map/pallas_call | solution.py:260
  131.5 1.5 copy.9
  133.0 0.0 copy-start
  133.0 1.4 slice_bitcast_fusion.ht
  134.4 1.9 %slice_bitcast_fusion.1 = (bf16[256,2048]{1,0:T(8,128)(2,1)S(1)}, bf16[256,2048]{1,0:T(8,128)(2,1)S(1)}) fusion(bf16[3,256,2048]{2,1,0:T(8,128)(2,1)} %get-tuple-element.10), kind=kLoop, calls=%fused_computation.2 | loop fusion | bytes 4194304 | tf_op jit(solution)/shard_map/squeeze | solution.py:333
  136.3 0.0 copy-done
  136.3 10.9 %shard_map.85 = (bf16[2048,2048]{1,0:T(8,128)(2,1)}, bf16[2048,2048]{1,0:T(8,128)(2,1)}, bf16[2048,2048]{1,0:T(8,128)(2,1)}) custom-call(bf16[2048,256]{1,0:T(8,128)(2,1)S(1)} %bitcast.13, bf16[2048,256]{1,0:T(8,128)(2,1)S(1)} %slice_bitcast_fusion.ht, bf16[256,2048]{1,0:T(8,128)(2,1)S(1)} %get-tuple-element.17.gg, ...), custom_call_target="tpu_custom_call" | custom-call | flops 6442450944 | bytes 30408704 | tf_op jit(solution)/shard_map/pallas_call | solution.py:304
  147.2 21.2 %reduce-scatter.2.cloned.1.call-done = f32[32,2048]{1,0:T(8,128)} async-done(((f32[256,2048]{1,0:T(8,128)}), f32[32,2048]{1,0:T(8,128)}) %reduce-scatter.2.cloned.1.call-update) | async-done | bytes 262160 | tf_op jit(solution)/shard_map/reduce_scatter | solution.py:335
  168.4 1.6 convert_element_type.3
Async XLA Ops:
  7.2 161.3 %reduce-scatter.2.cloned.1.call-start = ((), (), s32[]{:S(2)}) async-start(), calls=%async_computation.1 | async-start | bytes 2359296 | tf_op jit(solution)/shard_map/reduce_scatter | solution.py:335
  117.9 6.2 %copy-start.1 = (bf16[3,256,2048]{2,1,0:T(8,128)(2,1)S(1)}, bf16[3,256,2048]{2,1,0:T(8,128)(2,1)}, u32[]{:S(2)}) copy-start(bf16[3,256,2048]{2,1,0:T(8,128)(2,1)} %get-tuple-element.10) | copy-start | bytes 9437188
  117.9 7.0 %copy-start.2 = (bf16[2048,2048]{1,0:T(8,128)(2,1)S(1)}, bf16[2048,2048]{1,0:T(8,128)(2,1)}, u32[]{:S(2)}) copy-start(bf16[2048,2048]{1,0:T(8,128)(2,1)} %wu_hbm.1) | copy-start | bytes 25165828
  133.0 3.3 %copy-start = (bf16[256,2048]{1,0:T(8,128)(2,1)S(1)}, bf16[256,2048]{1,0:T(8,128)(2,1)}, u32[]{:S(2)}) copy-start(bf16[256,2048]{1,0:T(8,128)(2,1)} %get-tuple-element.12.og) | copy-start | bytes 3145732
Sparse Core Ops, SparseCore 0:
  128.8 39.5 reduce-scatter.1
